TPU v7x, 32 devices: a whole 2x2x4 slice. The times are simulated.
32 devices in a mesh: box: 8 (over z, x), path: 4 (over y, core).
Axes of the slice: x: 2, y: 2, z: 4, core: 2. Of those that a mesh axis runs over, the one named last changes fastest.
Arguments:
- features: float32 [1024, 9, 128], P('box'), may hold values from -6 to 6
- positions: float32 [3, 1024], P(None, 'box'), may hold values from 0 to 96, as said below
- cotangent: bfloat16 [1024, 9, 128], P('box'), may hold values from -6 to 6
- weights: float32 [8, 8, 128], P('path'), may hold values from -2 to 2
- neighbours: int32 [16, 3], P('box'), may hold values from 0 to 3, as said below
- send_list: int32 [8, 2], P('box'), may hold values from 0 to 1, as said below
Outputs:
- grad_features: float32 [1024, 9, 128], P(('box', 'path'))
- grad_weights: float32 [8, 8, 128], P('path')
Inputs may be any that keep to these rules, and one draw needn't show every extreme that they name: `positions`: stored block s of box b has a place g = b * 2 + (a permutation of 0 to 1 within the box) along a chain; its atoms lie near the points of a grid of spacing 1.5 with 4 x 4 points across and 4 along the third coordinate, the first coordinate between 6 g and 6 g + 6, each moved by at most 0.35 in each coordinate. Blocks whose places differ by two or more have no atoms within 5 of each other. `neighbours`: row g lists the block itself (its stored index), the block one place before it and the block one place after it along the chain, as table indices: below 2 the box's own stored blocks, 2 the block received from the previous box (its last block along the chain), 3 the block received from the next box (its first block along the chain). The relation is symmetric. send_list[b, 0] is the stored index of the first block of box b's stretch of the chain and send_list[b, 1] that of the last.
All inputs are finite; a program needn't handle non-finite values.
Results may differ from a plain program's by a relative error of at most 0.0045.
Values may be sent and summed in bfloat16 or wider, within the bound.
A program may use at most 64 MiB of HBM per device.

v0:
```python
import math
import jax
import jax.numpy as jnp
from jax import lax
from jax.sharding import PartitionSpec as P

BASIS = 8
BLOCK = 64
NEIGHBOURS = 3
PATHS = 8
cutoff_radius = 5.0
edge_scale = 0.2
basis_width = 0.8
root_three = math.sqrt(3.0)
path_terms = [
    [(0, [(0, 0, 1.0)])],
    [(0, [(1, 1, 1.0), (2, 2, 1.0), (3, 3, 1.0)])],
    [(1, [(1, 0, 1.0)]), (2, [(2, 0, 1.0)]), (3, [(3, 0, 1.0)])],
    [(1, [(0, 1, 1.0)]), (2, [(0, 2, 1.0)]), (3, [(0, 3, 1.0)])],
    [
        (4, [(4, 0, 1.0)]),
        (5, [(5, 0, 1.0)]),
        (6, [(6, 0, 1.0)]),
        (7, [(7, 0, 1.0)]),
        (8, [(8, 0, 1.0)]),
    ],
    [
        (4, [(0, 4, 1.0)]),
        (5, [(0, 5, 1.0)]),
        (6, [(0, 6, 1.0)]),
        (7, [(0, 7, 1.0)]),
        (8, [(0, 8, 1.0)]),
    ],
    [
        (1, [(3, 2, 1.0), (2, 3, -1.0)]),
        (2, [(1, 3, 1.0), (3, 1, -1.0)]),
        (3, [(2, 1, 1.0), (1, 2, -1.0)]),
    ],
    [(0, [(4, 4, 1.0), (5, 5, 1.0), (6, 6, 1.0), (7, 7, 1.0), (8, 8, 1.0)])],
]


def with_halo(cells, sides, width):
    for axis, dim in sides:
        count = lax.axis_size(axis)
        ends = count - 1
        head = lax.slice_in_dim(cells, 0, width, axis=dim)
        tail = lax.slice_in_dim(cells, cells.shape[dim] - width, cells.shape[dim], axis=dim)
        cells = jnp.concatenate(
            [
                lax.ppermute(tail, axis, [(i, (i + 1) % count) for i in range(ends)]),
                cells,
                lax.ppermute(head, axis, [((i + 1) % count, i) for i in range(ends)]),
            ],
            axis=dim,
        )
    return cells


def edge_tensor(anchor, target):
    offset = target[:, None, :] - anchor[:, :, None]
    square = jnp.sum(offset * offset, axis=0)
    inside = square > 0.01
    distance = jnp.sqrt(jnp.where(inside, square, 1.0))
    direction = offset / distance[None]
    envelope = jnp.where(
        inside & (distance < cutoff_radius),
        0.5 * (jnp.cos(math.pi * distance / cutoff_radius) + 1.0),
        0.0,
    )
    centres = (jnp.arange(BASIS, dtype=jnp.float32) + 0.5) * (cutoff_radius / BASIS)
    radial = (
        jnp.exp(-jnp.square((distance[None] - centres[:, None, None]) / basis_width))
        * (edge_scale * envelope)[None]
    )
    eastward = direction[0]
    northward = direction[1]
    upward = direction[2]
    harmonics = jnp.stack(
        [
            jnp.ones_like(eastward),
            eastward,
            northward,
            upward,
            root_three * eastward * northward,
            root_three * northward * upward,
            0.5 * (3.0 * upward * upward - 1.0),
            root_three * eastward * upward,
            0.5 * root_three * (eastward * eastward - northward * northward),
        ]
    )
    return (harmonics[:, None] * radial[None]).astype(jnp.bfloat16)


def forward_terms(paths, weights, edge_table, rounded):
    source_rows = rounded.shape[0]
    target_rows = edge_table.shape[2]
    channels = rounded.shape[2]
    outputs = [jnp.zeros((target_rows, channels), jnp.float32) for output in range(9)]
    for weight_slot, path_number in enumerate(paths):
        for output, term_list in path_terms[path_number]:
            pieces = []
            stacked = []
            for harmonic, source, factor in term_list:
                signed = edge_table[harmonic] if factor > 0 else -edge_table[harmonic]
                pieces.append(signed.reshape(BASIS * target_rows, source_rows))
                stacked.append(rounded[:, source, :])
            product = jnp.dot(
                jnp.concatenate(pieces, axis=1),
                jnp.concatenate(stacked, axis=0),
                preferred_element_type=jnp.float32,
            )
            product = product.reshape(BASIS, target_rows, channels)
            outputs[output] = outputs[output] + jnp.sum(
                weights[weight_slot][:, None, :] * product, axis=0
            )
    return jnp.stack(outputs, axis=1)


def transpose_terms(paths, weights, edge_table, cotangent_rows, source_features):
    rows = source_features.shape[0]
    channels = source_features.shape[2]
    outputs = [jnp.zeros((rows, channels), jnp.float32) for output in range(9)]
    weight_parts = []
    for weight_slot, path_number in enumerate(paths):
        weight_part = jnp.zeros((BASIS, channels), jnp.float32)
        for output, term_list in path_terms[path_number]:
            for harmonic, source, factor in term_list:
                gathered = lax.dot_general(
                    edge_table[harmonic],
                    cotangent_rows[:, output, :],
                    (((1,), (0,)), ((), ())),
                    preferred_element_type=jnp.float32,
                )
                outputs[source] = outputs[source] + factor * jnp.sum(
                    weights[weight_slot][:, None, :] * gathered, axis=0
                )
                weight_part = weight_part + factor * jnp.sum(
                    source_features[:, source, :][None] * gathered, axis=1
                )
        weight_parts.append(weight_part)
    return (jnp.stack(outputs, axis=1), jnp.stack(weight_parts, axis=0))


def gate_back(message, cotangent):
    incoming = cotangent.astype(jnp.float32)
    scalar = message[:, 0]
    sigma = jax.nn.sigmoid(scalar)
    slope = sigma * (1.0 + scalar * (1.0 - sigma))
    coupling = jnp.sum(incoming[:, 1:] * message[:, 1:], axis=1)
    leading = incoming[:, 0] * slope + sigma * (1.0 - sigma) * coupling
    others = incoming[:, 1:] * sigma[:, None]
    return jnp.concatenate([leading[:, None], others], axis=1).astype(jnp.bfloat16)


def on_device(features, positions, cotangent, weights, neighbours, send_list):
    local_blocks = neighbours.shape[0]
    local_rows = features.shape[0]
    channels = features.shape[2]
    block_features = features.reshape(local_blocks, BLOCK, 9, channels)
    block_places = positions.reshape(3, local_blocks, BLOCK).transpose(1, 0, 2)
    outgoing = send_list[0]
    padded_features, padded_places = (
        with_halo(block_features[outgoing], (("box", 0),), 1),
        with_halo(block_places[outgoing], (("box", 0),), 1),
    )
    table_features = jnp.concatenate(
        [block_features, padded_features[:1], padded_features[3:]], axis=0
    )
    table_places = jnp.concatenate([block_places, padded_places[:1], padded_places[3:]], axis=0)
    table_rounded = table_features.astype(jnp.bfloat16)
    group = lax.axis_index("path")
    share_rows = local_rows // lax.axis_size("path")
    cotangent_share = lax.dynamic_slice_in_dim(cotangent, group * share_rows, share_rows, 0)
    all_weights = lax.all_gather(weights, "path", axis=0, tiled=True)
    all_paths = list(range(PATHS))
    slab_rows = math.gcd(share_rows, BLOCK)
    slab_numbers = jnp.arange(share_rows // slab_rows, dtype=jnp.int32)

    def slab_anchor(slab_index):
        first_row = group * share_rows + slab_index * slab_rows
        block_number = first_row // BLOCK
        within_row = first_row % BLOCK
        anchor_rows = lax.dynamic_slice_in_dim(block_places[block_number], within_row, slab_rows, 1)
        return (block_number, within_row, anchor_rows)

    def forward_slab(slab_index):
        block_number, within_row, anchor_rows = slab_anchor(slab_index)
        total = jnp.zeros((slab_rows, 9, channels), jnp.float32)
        for neighbour in range(NEIGHBOURS):
            table_slot = neighbours[block_number, neighbour]
            edge_table = edge_tensor(anchor_rows, table_places[table_slot])
            total = total + forward_terms(
                all_paths, all_weights, edge_table, table_rounded[table_slot]
            )
        return total

    message_rows = lax.map(forward_slab, slab_numbers).reshape(share_rows, 9, channels)
    gate_rows = gate_back(message_rows, cotangent_share)
    message_cotangent = lax.all_gather(gate_rows, "path", axis=0, tiled=True)
    cotangent_blocks = message_cotangent.reshape(local_blocks, BLOCK, 9, channels)
    padded_gate = with_halo(cotangent_blocks[outgoing], (("box", 0),), 1)
    table_gate = jnp.concatenate([cotangent_blocks, padded_gate[:1], padded_gate[3:]], axis=0)

    def pull_slab(slab_index):
        block_number, within_row, anchor_rows = slab_anchor(slab_index)
        own_features = lax.dynamic_slice_in_dim(
            block_features[block_number], within_row, slab_rows, 0
        )
        total = jnp.zeros((slab_rows, 9, channels), jnp.float32)
        weight_total = jnp.zeros((PATHS, BASIS, channels), jnp.float32)
        for neighbour in range(NEIGHBOURS):
            table_slot = neighbours[block_number, neighbour]
            edge_table = edge_tensor(table_places[table_slot], anchor_rows)
            contribution, weight_part = transpose_terms(
                all_paths, all_weights, edge_table, table_gate[table_slot], own_features
            )
            total = total + contribution
            weight_total = weight_total + weight_part
        return (total, weight_total)

    totals, slab_weights = lax.map(pull_slab, slab_numbers)
    grad_features = totals.reshape(share_rows, 9, channels) + cotangent_share.astype(jnp.float32)
    weight_every = lax.psum(jnp.sum(slab_weights, axis=0), ("box", "path"))
    group_paths = PATHS // lax.axis_size("path")
    weight_total = lax.dynamic_slice_in_dim(weight_every, group * group_paths, group_paths, 0)
    return (grad_features, weight_total / math.sqrt(local_rows * lax.axis_size("box")))


def solution(mesh):
    placed = (
        P("box", None, None),
        P(None, "box"),
        P("box", None, None),
        P("path", None, None),
        P("box", None),
        P("box", None),
    )
    return jax.shard_map(
        on_device,
        mesh=mesh,
        in_specs=placed,
        out_specs=(P(("box", "path"), None, None), P("path", None, None)),
        check_vma=False,
    )
```

profile of v0, /device:TPU:0, one launch (start us, length us, event | category | flops | bytes accessed | tf_op | source)
XLA Modules:
  0.0 147.7 jit_solution(1303785314537078605)
XLA Ops:
  0.6 0.8 reshape.2374
  1.4 0.7 fusion.347
  2.6 4.9 %collective-permute-start = (f32[1,3,64]{2,1,0:T(4,128)S(1)}, f32[1,3,64]{2,1,0:T(4,128)S(1)}, u32[]{:S(2)}, u32[]{:S(2)}) collective-permute-start(f32[1,3,64]{2,1,0:T(4,128)S(1)} %get-tuple-element.590), channel_id=1, source_target_pairs={{0,4},{4,8},{8,12},{12,16},{16,20},{20,24},{24,28},{1,5},{5,9},{9,... | collective-permute-start | bytes 2312 | tf_op jit(solution)/shard_map/ppermute | solution.py:51
  7.5 1.3 collective-permute-start.1
  8.8 1.7 %gather_fusion.1 = bf16[2,64,9,128]{3,1,2,0:T(8,128)(2,1)S(1)} fusion(f32[2,64,9,128]{3,1,0,2:T(8,128)} %bitcast.899, s32[1024]{0:T(1024)S(1)} %pad_clamp_fusion), kind=kCustom, calls=%fused_computation.1 | custom fusion | bytes 589832 | tf_op jit(solution)/shard_map/gather | solution.py:164
  10.5 0.7 fusion.388
  11.3 5.2 %collective-permute-start.2 = (bf16[1,64,9,128]{3,1,2,0:T(8,128)(2,1)}, bf16[1,64,9,128]{3,1,2,0:T(8,128)(2,1)}, u32[]{:S(2)}, u32[]{:S(2)}) collective-permute-start(bf16[1,64,9,128]{3,1,2,0:T(8,128)(2,1)} %get-tuple-element.509), channel_id=1, source_target_pairs={{0,4},{4,8},{8,12},{12,16},{16,20},{20,24},{24,28},{1,5},{5,9},{9,... | collective-permute-start | bytes 442376 | tf_op jit(solution)/shard_map/ppermute | solution.py:51
  16.5 1.3 collective-permute-start.3
  18.0 0.7 constant_dynamic-slice_fusion.3
  20.0 5.2 %all_gather.6 = f32[8,8,128]{2,1,0:T(8,128)S(1)} all-gather(f32[2,8,128]{2,1,0:T(8,128)S(1)} %copy-done.55), channel_id=1, replica_groups=mesh['box'=8,'path'=4] {'path'}, dimensions={0}, use_global_device_ids=true | all-gather | bytes 40960 | tf_op jit(solution)/shard_map/all_gather | solution.py:175
  25.8 0.7 slice_bitcast_fusion.96
  26.4 1.6 %dynamic-slice_convert_fusion = f32[32,9,128]{2,0,1:T(8,128)} fusion(bf16[128,9,128]{2,0,1:T(8,128)(2,1)} %param.8, s32[]{:T(128)S(6)} %select_n.212), kind=kLoop, calls=%fused_computation.489 | loop fusion | flops 36864 | bytes 221188 | tf_op jit(solution)/shard_map/convert_element_type | solution.py:146
  33.4 0.8 fusion.384
  34.3 0.7 fusion.385
  35.3 0.8 fusion.386
  36.1 0.7 bitcast_negate_fusion.7
  42.8 0.8 copy-done.33
  43.7 1.8 %concatenate.157 = bf16[256,320]{1,0:T(8,128)(2,1)} concatenate(bf16[256,64]{1,0:T(8,128)(2,1)} %bitcast.946, bf16[256,64]{1,0:T(8,128)(2,1)} %bitcast.945, bf16[256,64]{1,0:T(8,128)(2,1)} %bitcast.944, bf16[256,64]{1,0:T(8,128)(2,1)} %bitcast.943, bf16[256,64]{1,0:T(8,128)(2,1)} %bitcast.942), dimensions={1} | concatenate | bytes 327680 | tf_op jit(solution)/shard_map/while/body/eval_jaxpr/concatenate | solution.py:109
  45.4 1.8 %concatenate.167 = bf16[256,320]{1,0:T(8,128)(2,1)} concatenate(bf16[256,64]{1,0:T(8,128)(2,1)} %bitcast.941, bf16[256,64]{1,0:T(8,128)(2,1)} %bitcast.940, bf16[256,64]{1,0:T(8,128)(2,1)} %bitcast.939, bf16[256,64]{1,0:T(8,128)(2,1)} %bitcast.938, bf16[256,64]{1,0:T(8,128)(2,1)} %bitcast.937), dimensions={1} | concatenate | bytes 327680 | tf_op jit(solution)/shard_map/while/body/eval_jaxpr/concatenate | solution.py:109
  47.2 1.8 %concatenate.147 = bf16[256,320]{1,0:T(8,128)(2,1)} concatenate(bf16[256,64]{1,0:T(8,128)(2,1)} %bitcast.936, bf16[256,64]{1,0:T(8,128)(2,1)} %bitcast.935, bf16[256,64]{1,0:T(8,128)(2,1)} %bitcast.934, bf16[256,64]{1,0:T(8,128)(2,1)} %bitcast.933, bf16[256,64]{1,0:T(8,128)(2,1)} %bitcast.932), dimensions={1} | concatenate | bytes 327680 | tf_op jit(solution)/shard_map/while/body/eval_jaxpr/concatenate | solution.py:109
  49.0 0.8 bitcast_negate_fusion.5
  49.8 1.1 pad_maximum_fusion
  51.1 0.9 copy-done.2
  64.9 0.7 copy-done.3
  65.7 6.0 %all_gather.7 = bf16[128,9,128]{2,0,1:T(8,128)(2,1)S(1)} all-gather(bf16[32,9,128]{2,0,1:T(8,128)(2,1)S(1)} %pad_maximum_fusion.1), channel_id=1, replica_groups=mesh['box'=8,'path'=4] {'path'}, dimensions={0}, use_global_device_ids=true | all-gather | bytes 368640 | tf_op jit(solution)/shard_map/all_gather | solution.py:200
  71.8 0.7 gather_fusion.2
  72.5 4.6 %collective-permute-start.4 = (bf16[1,64,9,128]{3,1,2,0:T(8,128)(2,1)S(1)}, bf16[1,64,9,128]{3,1,2,0:T(8,128)(2,1)S(1)}, u32[]{:S(2)}, u32[]{:S(2)}) collective-permute-start(bf16[1,64,9,128]{3,1,2,0:T(8,128)(2,1)S(1)} %get-tuple-element.508), channel_id=1, source_target_pairs={{0,4},{4,8},{8,12},{12,16},{16,20},{20,24},{24,28},{1,5},{5,9},{9,... | collective-permute-start | bytes 442376 | tf_op jit(solution)/shard_map/ppermute | solution.py:51
  77.1 1.5 collective-permute-start.5
  78.6 2.1 %collective-permute-done.4 = bf16[1,64,9,128]{3,1,2,0:T(8,128)(2,1)S(1)} collective-permute-done((bf16[1,64,9,128]{3,1,2,0:T(8,128)(2,1)S(1)}, bf16[1,64,9,128]{3,1,2,0:T(8,128)(2,1)S(1)}, u32[]{:S(2)}, u32[]{:S(2)}) %collective-permute-start.4) | collective-permute-done | bytes 147488 | tf_op jit(solution)/shard_map/ppermute | solution.py:51
  80.7 5.1 %collective-permute-done.5 = bf16[1,64,9,128]{3,1,2,0:T(8,128)(2,1)S(1)} collective-permute-done((bf16[1,64,9,128]{3,1,2,0:T(8,128)(2,1)S(1)}, bf16[1,64,9,128]{3,1,2,0:T(8,128)(2,1)S(1)}, u32[]{:S(2)}, u32[]{:S(2)}) %collective-permute-start.5) | collective-permute-done | bytes 147488 | tf_op jit(solution)/shard_map/ppermute | solution.py:53
  103.4 41.7 %psum.7 = f32[8,8,128]{2,1,0:T(8,128)S(1)} all-reduce(f32[8,8,128]{2,1,0:T(8,128)S(1)} %add_add_fusion.2), channel_id=1, replica_groups=mesh['box'=8,'path'=4] {'box','path'}, use_global_device_ids=true, to_apply=%region_259.260 | all-reduce | flops 8192 | bytes 65536 | tf_op jit(solution)/shard_map/psum | solution.py:224
  146.1 1.6 %add_add_fusion = f32[32,9,128]{2,0,1:T(8,128)} fusion(f32[32,9,128]{2,0,1:T(8,128)S(1)} %constant_dynamic-update-slice_fusion.104, f32[32,9,128]{2,0,1:T(8,128)S(1)} %constant_dynamic-update-slice_fusion.72, f32[32,9,128]{2,0,1:T(8,128)S(1)} %constant_dynamic-update-slice_fusion.88, bf16[128,9,128]{2,0,1:T(8,128)(2,1)} %param.8, s32[]{:T(128)S(6)} %select_n.212), kind=kLoop, calls=%fused_computation.252 | loop fusion | flops 147456 | bytes 663556 | tf_op jit(solution)/shard_map/add | solution.py:223
  (457 shorter events, 38.2 us)
Async XLA Ops:
  2.1 9.2 %copy-start.56 = (s32[1024]{0:T(1024)}, s32[1024]{0:T(1024)S(1)}, u32[]{:S(2)}) copy-start(s32[1024]{0:T(1024)S(1)} %pad_clamp_fusion) | copy-start | bytes 12292
  2.6 29.8 %collective-permute-start = (f32[1,3,64]{2,1,0:T(4,128)S(1)}, f32[1,3,64]{2,1,0:T(4,128)S(1)}, u32[]{:S(2)}, u32[]{:S(2)}) collective-permute-start(f32[1,3,64]{2,1,0:T(4,128)S(1)} %get-tuple-element.590), channel_id=1, source_target_pairs={{0,4},{4,8},{8,12},{12,16},{16,20},{20,24},{24,28},{1,5},{5,9},{9,... | collective-permute-start | bytes 2312 | tf_op jit(solution)/shard_map/ppermute | solution.py:51
  7.5 24.9 %collective-permute-start.1 = (f32[1,3,64]{2,1,0:T(4,128)S(1)}, f32[1,3,64]{2,1,0:T(4,128)S(1)}, u32[]{:S(2)}, u32[]{:S(2)}) collective-permute-start(f32[1,3,64]{2,1,0:T(4,128)S(1)} %get-tuple-element.591), channel_id=1, source_target_pairs={{4,0},{8,4},{12,8},{16,12},{20,16},{24,20},{28,24},{5,1},{9,5},{13... | collective-permute-start | bytes 2312 | tf_op jit(solution)/shard_map/ppermute | solution.py:53
  10.5 7.5 %copy-start = (f32[128,9,128]{2,0,1:T(8,128)S(1)}, f32[128,9,128]{2,0,1:T(8,128)}, u32[]{:S(2)}) copy-start(f32[128,9,128]{2,0,1:T(8,128)} %param.6) | copy-start | bytes 1769476
  10.5 7.5 %copy-start.57 = (s32[2,3]{1,0:T(2,128)S(1)}, s32[2,3]{1,0:T(2,128)}, u32[]{:S(2)}) copy-start(s32[2,3]{1,0:T(2,128)} %param.10) | copy-start | bytes 76
  10.5 9.5 %copy-start.55 = (f32[2,8,128]{2,1,0:T(8,128)S(1)}, f32[2,8,128]{2,1,0:T(8,128)}, u32[]{:S(2)}) copy-start(f32[2,8,128]{2,1,0:T(8,128)} %param.9) | copy-start | bytes 24580
  11.3 38.5 %collective-permute-start.2 = (bf16[1,64,9,128]{3,1,2,0:T(8,128)(2,1)}, bf16[1,64,9,128]{3,1,2,0:T(8,128)(2,1)}, u32[]{:S(2)}, u32[]{:S(2)}) collective-permute-start(bf16[1,64,9,128]{3,1,2,0:T(8,128)(2,1)} %get-tuple-element.509), channel_id=1, source_target_pairs={{0,4},{4,8},{8,12},{12,16},{16,20},{20,24},{24,28},{1,5},{5,9},{9,... | collective-permute-start | bytes 442376 | tf_op jit(solution)/shard_map/ppermute | solution.py:51
  16.5 33.4 %collective-permute-start.3 = (bf16[1,64,9,128]{3,1,2,0:T(8,128)(2,1)}, bf16[1,64,9,128]{3,1,2,0:T(8,128)(2,1)}, u32[]{:S(2)}, u32[]{:S(2)}) collective-permute-start(bf16[1,64,9,128]{3,1,2,0:T(8,128)(2,1)} %get-tuple-element.510), channel_id=1, source_target_pairs={{4,0},{8,4},{12,8},{16,12},{20,16},{24,20},{28,24},{5,1},{9,5},{13... | collective-permute-start | bytes 442376 | tf_op jit(solution)/shard_map/ppermute | solution.py:53
  34.1 2.0 %copy-start.9 = (bf16[1,8,32,64]{3,2,1,0:T(8,128)(2,1)}, bf16[1,8,32,64]{3,2,1,0:T(8,128)(2,1)S(1)}, u32[]{:S(2)}) copy-start(bf16[1,8,32,64]{3,2,1,0:T(8,128)(2,1)S(1)} %get-tuple-element.487) | copy-start | bytes 98308
  34.1 5.9 %copy-start.7 = (bf16[1,8,32,64]{3,2,1,0:T(8,128)(2,1)}, bf16[1,8,32,64]{3,2,1,0:T(8,128)(2,1)S(1)}, u32[]{:S(2)}) copy-start(bf16[1,8,32,64]{3,2,1,0:T(8,128)(2,1)S(1)} %get-tuple-element.480) | copy-start | bytes 98308
  34.1 6.5 %copy-start.11 = (bf16[1,8,32,64]{3,2,1,0:T(8,128)(2,1)}, bf16[1,8,32,64]{3,2,1,0:T(8,128)(2,1)S(1)}, u32[]{:S(2)}) copy-start(bf16[1,8,32,64]{3,2,1,0:T(8,128)(2,1)S(1)} %get-tuple-element.486) | copy-start | bytes 98308
  35.1 1.7 %copy-start.17 = (bf16[1,8,32,64]{3,2,1,0:T(8,128)(2,1)}, bf16[1,8,32,64]{3,2,1,0:T(8,128)(2,1)S(1)}, u32[]{:S(2)}) copy-start(bf16[1,8,32,64]{3,2,1,0:T(8,128)(2,1)S(1)} %get-tuple-element.488) | copy-start | bytes 98308
  35.1 2.3 %copy-start.15 = (bf16[1,8,32,64]{3,2,1,0:T(8,128)(2,1)}, bf16[1,8,32,64]{3,2,1,0:T(8,128)(2,1)S(1)}, u32[]{:S(2)}) copy-start(bf16[1,8,32,64]{3,2,1,0:T(8,128)(2,1)S(1)} %get-tuple-element.494) | copy-start | bytes 98308
  35.1 3.0 %copy-start.19 = (bf16[1,8,32,64]{3,2,1,0:T(8,128)(2,1)}, bf16[1,8,32,64]{3,2,1,0:T(8,128)(2,1)S(1)}, u32[]{:S(2)}) copy-start(bf16[1,8,32,64]{3,2,1,0:T(8,128)(2,1)S(1)} %get-tuple-element.495) | copy-start | bytes 98308
  35.3 1.5 %copy-start.1 = (bf16[9,8,32,64]{3,2,1,0:T(8,128)(2,1)}, bf16[9,8,32,64]{3,2,1,0:T(8,128)(2,1)S(1)}, u32[]{:S(2)}) copy-start(bf16[9,8,32,64]{3,2,1,0:T(8,128)(2,1)S(1)} %multiply_convert_fusion.3) | copy-start | bytes 884740
  36.1 5.4 %copy-start.13 = (bf16[1,8,32,64]{3,2,1,0:T(8,128)(2,1)}, bf16[1,8,32,64]{3,2,1,0:T(8,128)(2,1)S(1)}, u32[]{:S(2)}) copy-start(bf16[1,8,32,64]{3,2,1,0:T(8,128)(2,1)S(1)} %get-tuple-element.503) | copy-start | bytes 98308
  36.1 5.4 %copy-start.21 = (bf16[1,8,32,64]{3,2,1,0:T(8,128)(2,1)}, bf16[1,8,32,64]{3,2,1,0:T(8,128)(2,1)S(1)}, u32[]{:S(2)}) copy-start(bf16[1,8,32,64]{3,2,1,0:T(8,128)(2,1)S(1)} %get-tuple-element.502) | copy-start | bytes 98308
  50.9 1.1 copy-start.2
  50.9 1.1 copy-start.51
  50.9 1.3 copy-start.39
  51.0 1.9 %copy-start.49 = (f32[8,128]{1,0:T(8,128)S(1)}, f32[8,128]{1,0:T(8,128)}, u32[]{:S(2)}) copy-start(f32[8,128]{1,0:T(8,128)} %get-tuple-element.532) | copy-start | bytes 12292
  52.0 1.2 copy-start.37
  53.2 1.2 copy-start.53
  59.0 1.0 copy-start.20
  59.0 1.0 copy-start.31
  59.9 1.0 copy-start.29
  60.2 1.1 copy-start.14
  60.2 1.1 copy-start.22
  62.2 1.0 copy-start.4
  63.0 1.0 copy-start.6
  72.5 8.2 %collective-permute-start.4 = (bf16[1,64,9,128]{3,1,2,0:T(8,128)(2,1)S(1)}, bf16[1,64,9,128]{3,1,2,0:T(8,128)(2,1)S(1)}, u32[]{:S(2)}, u32[]{:S(2)}) collective-permute-start(bf16[1,64,9,128]{3,1,2,0:T(8,128)(2,1)S(1)} %get-tuple-element.508), channel_id=1, source_target_pairs={{0,4},{4,8},{8,12},{12,16},{16,20},{20,24},{24,28},{1,5},{5,9},{9,... | collective-permute-start | bytes 442376 | tf_op jit(solution)/shard_map/ppermute | solution.py:51
  77.1 8.7 %collective-permute-start.5 = (bf16[1,64,9,128]{3,1,2,0:T(8,128)(2,1)S(1)}, bf16[1,64,9,128]{3,1,2,0:T(8,128)(2,1)S(1)}, u32[]{:S(2)}, u32[]{:S(2)}) collective-permute-start(bf16[1,64,9,128]{3,1,2,0:T(8,128)(2,1)S(1)} %get-tuple-element.507), channel_id=1, source_target_pairs={{4,0},{8,4},{12,8},{16,12},{20,16},{24,20},{28,24},{5,1},{9,5},{13... | collective-permute-start | bytes 442376 | tf_op jit(solution)/shard_map/ppermute | solution.py:53
  (32 other events, 26.1 us)
where the time goes:
time: 149 us; the launch traced here: 148 us
  blocking collectives  53 us (36%)
  matrix products  25 us (17%)
  local copies, waits for them, and re-layouts  20.3 us (14%)
  starting transfers between devices  18.7 us (13%)
  other arithmetic  14.5 us (10%)
  between operations  9.16 us (6%)
  waiting for transfers between devices  7.16 us (5%)
    psum x1, blocking collectives, on_device(): weight_every = lax.psum(jnp.sum(slab_weights, axis=0), ('box', 'path'))  41.7 us
    ppermute x3, starting transfers between devices, with_halo(): lax.ppermute(tail, axis, [(i, (i + 1) % count) for i in range(ends)])  14.6 us
    dot_general x93, matrix products, transpose_terms(): lax.dot_general(edge_table[harmonic], cotangent_rows[:, output, :], (((1,...  14.4 us
    dot_general x66, matrix products, forward_terms(): jnp.dot(jnp.concatenate(pieces, axis=1), jnp.concatenate(stacked, axis=0)...  10.6 us
    all_gather x1, blocking collectives, on_device(): message_cotangent = lax.all_gather(gate_rows, 'path', axis=0, tiled=True)  6.04 us
    unnamed x139, local copies, waits for them, and re-layouts  6.02 us
    neg x9, other arithmetic, forward_terms(): signed = edge_table[harmonic] if factor > 0 else -edge_table[harmonic]  6.01 us
    concatenate x3, local copies, waits for them, and re-layouts, forward_terms(): jnp.concatenate(pieces, axis=1)  5.3 us
  transfers between devices with their start and end apart: 6, of which 2 were waited for; matrix products, arithmetic and copies ran while one was open for 15% of the time, Pallas kernels for 0%

commit v1 on v0

--- a/solution.py
+++ b/solution.py
@@ -221,7 +221,7 @@
 
     totals, slab_weights = lax.map(pull_slab, slab_numbers)
     grad_features = totals.reshape(share_rows, 9, channels) + cotangent_share.astype(jnp.float32)
-    weight_every = lax.psum(jnp.sum(slab_weights, axis=0), ("box", "path"))
+    weight_every = jax.lax.psum(jax.lax.psum(jnp.sum(slab_weights, axis=0), "path"), "box")
     group_paths = PATHS // lax.axis_size("path")
     weight_total = lax.dynamic_slice_in_dim(weight_every, group * group_paths, group_paths, 0)
     return (grad_features, weight_total / math.sqrt(local_rows * lax.axis_size("box")))

time: 149 us -> 155 us (1.040)
  blocking collectives: 53 us -> 59.2 us
    psum x1 -> x2, blocking collectives: 41.7 us -> 48 us  [the longest x1 37.2 us: on_device(): jax.lax.psum(jax.lax.psum(jnp.sum(slab_weights, axis=0), 'path'), 'box')]
  transfers between devices with their start and end apart: 6 -> 6, of which waited for: 2 -> 2; matrix products, arithmetic and copies ran while one was open for 15% -> 14% of each run, Pallas kernels for 0% -> 0%
where the time goes in v1:
time: 155 us; the launch traced here: 154 us
  blocking collectives  59.2 us (38%)
  matrix products  25 us (16%)
  local copies, waits for them, and re-layouts  20.3 us (13%)
  starting transfers between devices  18.7 us (12%)
  other arithmetic  14.4 us (9%)
  between operations  9.16 us (6%)
  waiting for transfers between devices  7.16 us (5%)
    psum x1, blocking collectives, on_device(): jax.lax.psum(jax.lax.psum(jnp.sum(slab_weights, axis=0), 'path'), 'box')  37.2 us
    ppermute x3, starting transfers between devices, with_halo(): lax.ppermute(tail, axis, [(i, (i + 1) % count) for i in range(ends)])  14.6 us
    dot_general x93, matrix products, transpose_terms(): lax.dot_general(edge_table[harmonic], cotangent_rows[:, output, :], (((1,...  14.4 us
    psum x1, blocking collectives, on_device(): jax.lax.psum(jnp.sum(slab_weights, axis=0), 'path')  10.8 us
    dot_general x66, matrix products, forward_terms(): jnp.dot(jnp.concatenate(pieces, axis=1), jnp.concatenate(stacked, axis=0)...  10.6 us
    all_gather x1, blocking collectives, on_device(): message_cotangent = lax.all_gather(gate_rows, 'path', axis=0, tiled=True)  6.04 us
    unnamed x139, local copies, waits for them, and re-layouts  6.02 us
    neg x9, other arithmetic, forward_terms(): signed = edge_table[harmonic] if factor > 0 else -edge_table[harmonic]  6.01 us
  transfers between devices with their start and end apart: 6, of which 2 were waited for; matrix products, arithmetic and copies ran while one was open for 14% of the time, Pallas kernels for 0%

profile of v1, /device:TPU:0, one launch (start us, length us, event | category | flops | bytes accessed | tf_op | source)
XLA Modules:
  0.0 153.9 jit_solution(14197606802374449305)
XLA Ops:
  0.6 0.8 reshape.2374
  1.4 0.7 fusion.347
  2.6 4.9 %collective-permute-start = (f32[1,3,64]{2,1,0:T(4,128)S(1)}, f32[1,3,64]{2,1,0:T(4,128)S(1)}, u32[]{:S(2)}, u32[]{:S(2)}) collective-permute-start(f32[1,3,64]{2,1,0:T(4,128)S(1)} %get-tuple-element.590), channel_id=1, source_target_pairs={{0,4},{4,8},{8,12},{12,16},{16,20},{20,24},{24,28},{1,5},{5,9},{9,... | collective-permute-start | bytes 2312 | tf_op jit(solution)/shard_map/ppermute | solution.py:51
  7.5 1.3 collective-permute-start.1
  8.8 1.7 %gather_fusion.1 = bf16[2,64,9,128]{3,1,2,0:T(8,128)(2,1)S(1)} fusion(f32[2,64,9,128]{3,1,0,2:T(8,128)} %bitcast.899, s32[1024]{0:T(1024)S(1)} %pad_clamp_fusion), kind=kCustom, calls=%fused_computation.1 | custom fusion | bytes 589832 | tf_op jit(solution)/shard_map/gather | solution.py:164
  10.5 0.7 fusion.388
  11.3 5.2 %collective-permute-start.2 = (bf16[1,64,9,128]{3,1,2,0:T(8,128)(2,1)}, bf16[1,64,9,128]{3,1,2,0:T(8,128)(2,1)}, u32[]{:S(2)}, u32[]{:S(2)}) collective-permute-start(bf16[1,64,9,128]{3,1,2,0:T(8,128)(2,1)} %get-tuple-element.509), channel_id=1, source_target_pairs={{0,4},{4,8},{8,12},{12,16},{16,20},{20,24},{24,28},{1,5},{5,9},{9,... | collective-permute-start | bytes 442376 | tf_op jit(solution)/shard_map/ppermute | solution.py:51
  16.5 1.3 collective-permute-start.3
  18.0 0.7 constant_dynamic-slice_fusion.3
  20.0 5.2 %all_gather.6 = f32[8,8,128]{2,1,0:T(8,128)S(1)} all-gather(f32[2,8,128]{2,1,0:T(8,128)S(1)} %copy-done.55), channel_id=1, replica_groups=mesh['box'=8,'path'=4] {'path'}, dimensions={0}, use_global_device_ids=true | all-gather | bytes 40960 | tf_op jit(solution)/shard_map/all_gather | solution.py:175
  26.4 1.6 %dynamic-slice_convert_fusion = f32[32,9,128]{2,0,1:T(8,128)} fusion(bf16[128,9,128]{2,0,1:T(8,128)(2,1)} %param.8, s32[]{:T(128)S(6)} %select_n.212), kind=kLoop, calls=%fused_computation.489 | loop fusion | flops 36864 | bytes 221188 | tf_op jit(solution)/shard_map/convert_element_type | solution.py:146
  33.4 0.8 fusion.384
  34.3 0.7 fusion.385
  35.3 0.8 fusion.386
  36.1 0.7 bitcast_negate_fusion.7
  42.8 0.8 copy-done.33
  43.7 1.8 %concatenate.157 = bf16[256,320]{1,0:T(8,128)(2,1)} concatenate(bf16[256,64]{1,0:T(8,128)(2,1)} %bitcast.946, bf16[256,64]{1,0:T(8,128)(2,1)} %bitcast.945, bf16[256,64]{1,0:T(8,128)(2,1)} %bitcast.944, bf16[256,64]{1,0:T(8,128)(2,1)} %bitcast.943, bf16[256,64]{1,0:T(8,128)(2,1)} %bitcast.942), dimensions={1} | concatenate | bytes 327680 | tf_op jit(solution)/shard_map/while/body/eval_jaxpr/concatenate | solution.py:109
  45.4 1.8 %concatenate.167 = bf16[256,320]{1,0:T(8,128)(2,1)} concatenate(bf16[256,64]{1,0:T(8,128)(2,1)} %bitcast.941, bf16[256,64]{1,0:T(8,128)(2,1)} %bitcast.940, bf16[256,64]{1,0:T(8,128)(2,1)} %bitcast.939, bf16[256,64]{1,0:T(8,128)(2,1)} %bitcast.938, bf16[256,64]{1,0:T(8,128)(2,1)} %bitcast.937), dimensions={1} | concatenate | bytes 327680 | tf_op jit(solution)/shard_map/while/body/eval_jaxpr/concatenate | solution.py:109
  47.2 1.8 %concatenate.147 = bf16[256,320]{1,0:T(8,128)(2,1)} concatenate(bf16[256,64]{1,0:T(8,128)(2,1)} %bitcast.936, bf16[256,64]{1,0:T(8,128)(2,1)} %bitcast.935, bf16[256,64]{1,0:T(8,128)(2,1)} %bitcast.934, bf16[256,64]{1,0:T(8,128)(2,1)} %bitcast.933, bf16[256,64]{1,0:T(8,128)(2,1)} %bitcast.932), dimensions={1} | concatenate | bytes 327680 | tf_op jit(solution)/shard_map/while/body/eval_jaxpr/concatenate | solution.py:109
  49.0 0.8 bitcast_negate_fusion.5
  49.8 1.1 pad_maximum_fusion
  51.1 0.9 copy-done.2
  64.9 0.7 copy-done.3
  65.7 6.0 %all_gather.7 = bf16[128,9,128]{2,0,1:T(8,128)(2,1)S(1)} all-gather(bf16[32,9,128]{2,0,1:T(8,128)(2,1)S(1)} %pad_maximum_fusion.1), channel_id=1, replica_groups=mesh['box'=8,'path'=4] {'path'}, dimensions={0}, use_global_device_ids=true | all-gather | bytes 368640 | tf_op jit(solution)/shard_map/all_gather | solution.py:200
  71.8 0.7 gather_fusion.2
  72.5 4.6 %collective-permute-start.4 = (bf16[1,64,9,128]{3,1,2,0:T(8,128)(2,1)S(1)}, bf16[1,64,9,128]{3,1,2,0:T(8,128)(2,1)S(1)}, u32[]{:S(2)}, u32[]{:S(2)}) collective-permute-start(bf16[1,64,9,128]{3,1,2,0:T(8,128)(2,1)S(1)} %get-tuple-element.508), channel_id=1, source_target_pairs={{0,4},{4,8},{8,12},{12,16},{16,20},{20,24},{24,28},{1,5},{5,9},{9,... | collective-permute-start | bytes 442376 | tf_op jit(solution)/shard_map/ppermute | solution.py:51
  77.1 1.5 collective-permute-start.5
  78.6 2.1 %collective-permute-done.4 = bf16[1,64,9,128]{3,1,2,0:T(8,128)(2,1)S(1)} collective-permute-done((bf16[1,64,9,128]{3,1,2,0:T(8,128)(2,1)S(1)}, bf16[1,64,9,128]{3,1,2,0:T(8,128)(2,1)S(1)}, u32[]{:S(2)}, u32[]{:S(2)}) %collective-permute-start.4) | collective-permute-done | bytes 147488 | tf_op jit(solution)/shard_map/ppermute | solution.py:51
  80.7 5.1 %collective-permute-done.5 = bf16[1,64,9,128]{3,1,2,0:T(8,128)(2,1)S(1)} collective-permute-done((bf16[1,64,9,128]{3,1,2,0:T(8,128)(2,1)S(1)}, bf16[1,64,9,128]{3,1,2,0:T(8,128)(2,1)S(1)}, u32[]{:S(2)}, u32[]{:S(2)}) %collective-permute-start.5) | collective-permute-done | bytes 147488 | tf_op jit(solution)/shard_map/ppermute | solution.py:53
  103.4 10.8 %psum.14 = f32[8,8,128]{2,1,0:T(8,128)S(1)} all-reduce(f32[8,8,128]{2,1,0:T(8,128)S(1)} %add_add_fusion.2), channel_id=1, replica_groups=mesh['box'=8,'path'=4] {'path'}, use_global_device_ids=true, to_apply=%region_259.260 | all-reduce | flops 8192 | bytes 65536 | tf_op jit(solution)/shard_map/psum | solution.py:224
  114.1 37.2 %psum.15 = f32[8,8,128]{2,1,0:T(8,128)S(1)} all-reduce(f32[8,8,128]{2,1,0:T(8,128)S(1)} %psum.14), channel_id=1, replica_groups=mesh['box'=8,'path'=4] {'box'}, use_global_device_ids=true, to_apply=%region_260.261 | all-reduce | flops 8192 | bytes 65536 | tf_op jit(solution)/shard_map/psum | solution.py:224
  152.3 1.6 %add_add_fusion = f32[32,9,128]{2,0,1:T(8,128)} fusion(f32[32,9,128]{2,0,1:T(8,128)S(1)} %constant_dynamic-update-slice_fusion.104, f32[32,9,128]{2,0,1:T(8,128)S(1)} %constant_dynamic-update-slice_fusion.72, f32[32,9,128]{2,0,1:T(8,128)S(1)} %constant_dynamic-update-slice_fusion.88, bf16[128,9,128]{2,0,1:T(8,128)(2,1)} %param.8, s32[]{:T(128)S(6)} %select_n.212), kind=kLoop, calls=%fused_computation.252 | loop fusion | flops 147456 | bytes 663556 | tf_op jit(solution)/shard_map/add | solution.py:223
  (458 shorter events, 38.8 us)
Async XLA Ops:
  2.1 9.2 %copy-start.56 = (s32[1024]{0:T(1024)}, s32[1024]{0:T(1024)S(1)}, u32[]{:S(2)}) copy-start(s32[1024]{0:T(1024)S(1)} %pad_clamp_fusion) | copy-start | bytes 12292
  2.6 29.8 %collective-permute-start = (f32[1,3,64]{2,1,0:T(4,128)S(1)}, f32[1,3,64]{2,1,0:T(4,128)S(1)}, u32[]{:S(2)}, u32[]{:S(2)}) collective-permute-start(f32[1,3,64]{2,1,0:T(4,128)S(1)} %get-tuple-element.590), channel_id=1, source_target_pairs={{0,4},{4,8},{8,12},{12,16},{16,20},{20,24},{24,28},{1,5},{5,9},{9,... | collective-permute-start | bytes 2312 | tf_op jit(solution)/shard_map/ppermute | solution.py:51
  7.5 24.9 %collective-permute-start.1 = (f32[1,3,64]{2,1,0:T(4,128)S(1)}, f32[1,3,64]{2,1,0:T(4,128)S(1)}, u32[]{:S(2)}, u32[]{:S(2)}) collective-permute-start(f32[1,3,64]{2,1,0:T(4,128)S(1)} %get-tuple-element.591), channel_id=1, source_target_pairs={{4,0},{8,4},{12,8},{16,12},{20,16},{24,20},{28,24},{5,1},{9,5},{13... | collective-permute-start | bytes 2312 | tf_op jit(solution)/shard_map/ppermute | solution.py:53
  10.5 7.5 %copy-start = (f32[128,9,128]{2,0,1:T(8,128)S(1)}, f32[128,9,128]{2,0,1:T(8,128)}, u32[]{:S(2)}) copy-start(f32[128,9,128]{2,0,1:T(8,128)} %param.6) | copy-start | bytes 1769476
  10.5 7.5 %copy-start.57 = (s32[2,3]{1,0:T(2,128)S(1)}, s32[2,3]{1,0:T(2,128)}, u32[]{:S(2)}) copy-start(s32[2,3]{1,0:T(2,128)} %param.10) | copy-start | bytes 76
  10.5 9.5 %copy-start.55 = (f32[2,8,128]{2,1,0:T(8,128)S(1)}, f32[2,8,128]{2,1,0:T(8,128)}, u32[]{:S(2)}) copy-start(f32[2,8,128]{2,1,0:T(8,128)} %param.9) | copy-start | bytes 24580
  11.3 38.5 %collective-permute-start.2 = (bf16[1,64,9,128]{3,1,2,0:T(8,128)(2,1)}, bf16[1,64,9,128]{3,1,2,0:T(8,128)(2,1)}, u32[]{:S(2)}, u32[]{:S(2)}) collective-permute-start(bf16[1,64,9,128]{3,1,2,0:T(8,128)(2,1)} %get-tuple-element.509), channel_id=1, source_target_pairs={{0,4},{4,8},{8,12},{12,16},{16,20},{20,24},{24,28},{1,5},{5,9},{9,... | collective-permute-start | bytes 442376 | tf_op jit(solution)/shard_map/ppermute | solution.py:51
  16.5 33.4 %collective-permute-start.3 = (bf16[1,64,9,128]{3,1,2,0:T(8,128)(2,1)}, bf16[1,64,9,128]{3,1,2,0:T(8,128)(2,1)}, u32[]{:S(2)}, u32[]{:S(2)}) collective-permute-start(bf16[1,64,9,128]{3,1,2,0:T(8,128)(2,1)} %get-tuple-element.510), channel_id=1, source_target_pairs={{4,0},{8,4},{12,8},{16,12},{20,16},{24,20},{28,24},{5,1},{9,5},{13... | collective-permute-start | bytes 442376 | tf_op jit(solution)/shard_map/ppermute | solution.py:53
  34.1 2.0 %copy-start.9 = (bf16[1,8,32,64]{3,2,1,0:T(8,128)(2,1)}, bf16[1,8,32,64]{3,2,1,0:T(8,128)(2,1)S(1)}, u32[]{:S(2)}) copy-start(bf16[1,8,32,64]{3,2,1,0:T(8,128)(2,1)S(1)} %get-tuple-element.487) | copy-start | bytes 98308
  34.1 5.9 %copy-start.7 = (bf16[1,8,32,64]{3,2,1,0:T(8,128)(2,1)}, bf16[1,8,32,64]{3,2,1,0:T(8,128)(2,1)S(1)}, u32[]{:S(2)}) copy-start(bf16[1,8,32,64]{3,2,1,0:T(8,128)(2,1)S(1)} %get-tuple-element.480) | copy-start | bytes 98308
  34.1 6.5 %copy-start.11 = (bf16[1,8,32,64]{3,2,1,0:T(8,128)(2,1)}, bf16[1,8,32,64]{3,2,1,0:T(8,128)(2,1)S(1)}, u32[]{:S(2)}) copy-start(bf16[1,8,32,64]{3,2,1,0:T(8,128)(2,1)S(1)} %get-tuple-element.486) | copy-start | bytes 98308
  35.1 1.7 %copy-start.17 = (bf16[1,8,32,64]{3,2,1,0:T(8,128)(2,1)}, bf16[1,8,32,64]{3,2,1,0:T(8,128)(2,1)S(1)}, u32[]{:S(2)}) copy-start(bf16[1,8,32,64]{3,2,1,0:T(8,128)(2,1)S(1)} %get-tuple-element.488) | copy-start | bytes 98308
  35.1 2.3 %copy-start.15 = (bf16[1,8,32,64]{3,2,1,0:T(8,128)(2,1)}, bf16[1,8,32,64]{3,2,1,0:T(8,128)(2,1)S(1)}, u32[]{:S(2)}) copy-start(bf16[1,8,32,64]{3,2,1,0:T(8,128)(2,1)S(1)} %get-tuple-element.494) | copy-start | bytes 98308
  35.1 3.0 %copy-start.19 = (bf16[1,8,32,64]{3,2,1,0:T(8,128)(2,1)}, bf16[1,8,32,64]{3,2,1,0:T(8,128)(2,1)S(1)}, u32[]{:S(2)}) copy-start(bf16[1,8,32,64]{3,2,1,0:T(8,128)(2,1)S(1)} %get-tuple-element.495) | copy-start | bytes 98308
  35.3 1.5 copy-start.1
  36.1 5.4 %copy-start.13 = (bf16[1,8,32,64]{3,2,1,0:T(8,128)(2,1)}, bf16[1,8,32,64]{3,2,1,0:T(8,128)(2,1)S(1)}, u32[]{:S(2)}) copy-start(bf16[1,8,32,64]{3,2,1,0:T(8,128)(2,1)S(1)} %get-tuple-element.503) | copy-start | bytes 98308
  36.1 5.4 %copy-start.21 = (bf16[1,8,32,64]{3,2,1,0:T(8,128)(2,1)}, bf16[1,8,32,64]{3,2,1,0:T(8,128)(2,1)S(1)}, u32[]{:S(2)}) copy-start(bf16[1,8,32,64]{3,2,1,0:T(8,128)(2,1)S(1)} %get-tuple-element.502) | copy-start | bytes 98308
  50.9 1.1 copy-start.2
  50.9 1.1 copy-start.51
  50.9 1.3 copy-start.39
  51.0 1.9 %copy-start.49 = (f32[8,128]{1,0:T(8,128)S(1)}, f32[8,128]{1,0:T(8,128)}, u32[]{:S(2)}) copy-start(f32[8,128]{1,0:T(8,128)} %get-tuple-element.532) | copy-start | bytes 12292
  52.0 1.2 copy-start.37
  53.2 1.2 copy-start.53
  59.0 1.0 copy-start.20
  59.0 1.0 copy-start.31
  59.9 1.0 copy-start.29
  60.2 1.1 copy-start.14
  60.2 1.1 copy-start.22
  62.2 1.0 copy-start.4
  63.0 1.0 copy-start.6
  72.5 8.2 %collective-permute-start.4 = (bf16[1,64,9,128]{3,1,2,0:T(8,128)(2,1)S(1)}, bf16[1,64,9,128]{3,1,2,0:T(8,128)(2,1)S(1)}, u32[]{:S(2)}, u32[]{:S(2)}) collective-permute-start(bf16[1,64,9,128]{3,1,2,0:T(8,128)(2,1)S(1)} %get-tuple-element.508), channel_id=1, source_target_pairs={{0,4},{4,8},{8,12},{12,16},{16,20},{20,24},{24,28},{1,5},{5,9},{9,... | collective-permute-start | bytes 442376 | tf_op jit(solution)/shard_map/ppermute | solution.py:51
  77.1 8.7 %collective-permute-start.5 = (bf16[1,64,9,128]{3,1,2,0:T(8,128)(2,1)S(1)}, bf16[1,64,9,128]{3,1,2,0:T(8,128)(2,1)S(1)}, u32[]{:S(2)}, u32[]{:S(2)}) collective-permute-start(bf16[1,64,9,128]{3,1,2,0:T(8,128)(2,1)S(1)} %get-tuple-element.507), channel_id=1, source_target_pairs={{4,0},{8,4},{12,8},{16,12},{20,16},{24,20},{28,24},{5,1},{9,5},{13... | collective-permute-start | bytes 442376 | tf_op jit(solution)/shard_map/ppermute | solution.py:53
  (32 other events, 26.1 us)
